TPU v7x, 32 devices: a whole 2x2x4 slice. The times are simulated.
32 devices in a mesh: expert: 8 (over z, x), fsdp: 4 (over y, core).
Axes of the slice: x: 2, y: 2, z: 4, core: 2. Of those that a mesh axis runs over, the one named last changes fastest.
Arguments:
- tokens: bfloat16 [2048, 7168], P('expert', 'fsdp'), may hold values from -6 to 6
- output_grad: bfloat16 [2048, 7168], P('expert', 'fsdp'), may hold values from -6 to 6
- route_weight: float32 [2048, 8], P('expert'), may hold values from 0.05 to 0.5
- expert_ids: int32 [2048, 8], P('expert'), may hold values from 0 to 255, all different within a row; in each aligned block of 256 rows (0 to 255, 256 to 511, ...) at most 12 rows name the same one
- gate_weight: bfloat16 [8, 7168, 512], P('expert', 'fsdp'), may hold values from -0.0625 to 0.0625
- up_weight: bfloat16 [8, 7168, 512], P('expert', 'fsdp'), may hold values from -0.0625 to 0.0625
- down_weight: bfloat16 [8, 512, 7168], P('expert', None, 'fsdp'), may hold values from -0.1875 to 0.1875
Outputs:
- token_grad: bfloat16 [2048, 7168], P('expert', 'fsdp')
- gate_grad: bfloat16 [8, 7168, 512], P('expert', 'fsdp')
- up_grad: bfloat16 [8, 7168, 512], P('expert', 'fsdp')
- down_grad: bfloat16 [8, 512, 7168], P('expert', None, 'fsdp')
Inputs may be any that keep to these rules, and one draw needn't show every extreme that they name: `expert_ids`: in each block of 256 rows (the tokens held by one position along `expert` (one block of 256 consecutive rows)) no expert is named by more than 12 rows, a bound that some block reaches.
All inputs are finite; a program needn't handle non-finite values.
Results may differ from a plain program's by a relative error of at most 0.025.
Values may be sent and summed in bfloat16 or wider, within the bound.
No kernel may reach another device: no remote copies, remote signals or barrier semaphores. Data moves between devices by JAX's collectives and lax.ppermute only.
A program may use at most 64 MiB of HBM per device.

v0:
```python
import jax
import jax.numpy as jnp
from jax import lax
from jax.sharding import PartitionSpec as P

CAP = 12


def swiglu_grads(gate, up_value, hidden_grad):
    sigmoid_gate = jax.nn.sigmoid(gate)
    activation = (gate * sigmoid_gate * up_value).astype(jnp.bfloat16)
    gate_delta = (
        hidden_grad * up_value * sigmoid_gate * (1.0 + gate * (1.0 - sigmoid_gate))
    ).astype(jnp.bfloat16)
    up_delta = (hidden_grad * gate * sigmoid_gate).astype(jnp.bfloat16)
    return (activation, gate_delta, up_delta)


def body(tokens, output_grad, route_weight, expert_ids, gate_weight, up_weight, down_weight):
    expert_count = lax.axis_size("expert")
    window = expert_count // 2
    tok_rows, top_count = expert_ids.shape
    slab_width = tokens.shape[1]
    slot_count = expert_count * CAP
    send_count = window * CAP
    in_window = expert_ids < window
    expert_hits = (
        expert_ids[:, :, None] == jnp.arange(window, dtype=jnp.int32)[None, None, :]
    ).astype(jnp.int32)
    flat_hits = expert_hits.reshape(tok_rows * top_count, window)
    earlier = jnp.cumsum(flat_hits, axis=0) - flat_hits
    slot_rank = jnp.sum(earlier * flat_hits, axis=1).reshape(tok_rows, top_count)
    slot_ids = jnp.where(in_window, expert_ids * CAP + slot_rank, -1)
    matches = slot_ids[None, :, :] == jnp.arange(send_count, dtype=jnp.int32)[:, None, None]
    placing = jnp.sum(matches.astype(jnp.float32), axis=2).astype(jnp.bfloat16)
    weighted = jnp.sum(jnp.where(matches, route_weight[None, :, :], 0.0), axis=2)
    sent_rows = jnp.dot(placing, tokens, preferred_element_type=jnp.float32).astype(jnp.bfloat16)
    sent_grads = jnp.dot(
        weighted, output_grad.astype(jnp.float32), precision=lax.Precision.HIGHEST
    ).astype(jnp.bfloat16)
    paired_rows = jnp.repeat(sent_rows.reshape(window, CAP, slab_width), 2, axis=0)
    paired_grads = jnp.repeat(sent_grads.reshape(window, CAP, slab_width), 2, axis=0)
    recv_rows, recv_grads = (
        lax.all_to_all(paired_rows, "expert", split_axis=0, concat_axis=0, tiled=True),
        lax.all_to_all(paired_grads, "expert", split_axis=0, concat_axis=0, tiled=True),
    )
    rows = recv_rows.reshape(slot_count, slab_width)
    grads = recv_grads.reshape(slot_count, slab_width)
    gate_w = gate_weight[0]
    up_w = up_weight[0]
    down_w = down_weight[0]
    hidden_width = gate_w.shape[1]
    over_rows = (((0,), (0,)), ((), ()))
    over_columns = (((1,), (1,)), ((), ()))
    gate_part = jnp.dot(rows, gate_w, preferred_element_type=jnp.float32)
    up_part = jnp.dot(rows, up_w, preferred_element_type=jnp.float32)
    hidden_part = lax.dot_general(grads, down_w, over_columns, preferred_element_type=jnp.float32)
    gate_sum, up_sum = (
        lax.psum(gate_part.astype(jnp.bfloat16), "fsdp").astype(jnp.float32),
        lax.psum(up_part.astype(jnp.bfloat16), "fsdp").astype(jnp.float32),
    )
    hidden_share = lax.psum_scatter(
        hidden_part.astype(jnp.bfloat16), "fsdp", scatter_dimension=1, tiled=True
    ).astype(jnp.float32)
    share_width = hidden_width // lax.axis_size("fsdp")
    share_start = lax.axis_index("fsdp") * share_width
    gate_share = lax.dynamic_slice_in_dim(gate_sum, share_start, share_width, 1)
    up_share = lax.dynamic_slice_in_dim(up_sum, share_start, share_width, 1)
    activation = (gate_sum * jax.nn.sigmoid(gate_sum) * up_sum).astype(jnp.bfloat16)
    unused, gate_piece, up_piece = swiglu_grads(gate_share, up_share, hidden_share)
    gate_delta, up_delta = (
        lax.all_gather(gate_piece, "fsdp", axis=1, tiled=True),
        lax.all_gather(up_piece, "fsdp", axis=1, tiled=True),
    )
    down_grad = lax.dot_general(
        activation, grads, over_rows, preferred_element_type=jnp.float32
    ).astype(jnp.bfloat16)
    gate_grad = lax.dot_general(
        rows, gate_delta, over_rows, preferred_element_type=jnp.float32
    ).astype(jnp.bfloat16)
    up_grad = lax.dot_general(rows, up_delta, over_rows, preferred_element_type=jnp.float32).astype(
        jnp.bfloat16
    )
    back_rows = lax.dot_general(
        gate_delta, gate_w, over_columns, preferred_element_type=jnp.float32
    )
    back_rows = (
        back_rows
        + lax.dot_general(up_delta, up_w, over_columns, preferred_element_type=jnp.float32)
    ).astype(jnp.bfloat16)
    returned = lax.all_to_all(
        back_rows.reshape(expert_count, CAP, slab_width),
        "expert",
        split_axis=0,
        concat_axis=0,
        tiled=True,
    )
    halves = returned.reshape(window, 2, CAP, slab_width)
    first_half = halves[:, 0].reshape(send_count, slab_width)
    second_half = halves[:, 1].reshape(send_count, slab_width)
    token_total = lax.dot_general(
        placing, first_half, over_rows, preferred_element_type=jnp.float32
    )
    token_total = token_total + lax.dot_general(
        placing, second_half, over_rows, preferred_element_type=jnp.float32
    )
    token_grad = token_total.astype(jnp.bfloat16)
    return (token_grad, gate_grad[None], up_grad[None], down_grad[None])


def solution(mesh):
    placed = (
        P("expert", "fsdp"),
        P("expert", "fsdp"),
        P("expert", None),
        P("expert", None),
        P("expert", "fsdp", None),
        P("expert", "fsdp", None),
        P("expert", None, "fsdp"),
    )
    return jax.shard_map(
        body,
        mesh=mesh,
        in_specs=placed,
        out_specs=(
            P("expert", "fsdp"),
            P("expert", "fsdp", None),
            P("expert", "fsdp", None),
            P("expert", None, "fsdp"),
        ),
        check_vma=False,
    )
```

profile of v0, /device:TPU:0, one launch (start us, length us, event | category | flops | bytes accessed | tf_op | source)
XLA Modules:
  0.0 140.8 jit_solution(10445876984155720721)
XLA Ops:
  7.2 1.0 copy.40
  8.4 1.2 reduce-window.6
  10.9 0.9 convert_reduce_fusion
  11.9 1.5 %convolution_convert_fusion.3 = bf16[48,1792]{1,0:T(8,128)(2,1)S(1)} fusion(bf16[256,1792]{1,0:T(8,128)(2,1)} %param.7, bf16[48,256]{1,0:T(8,128)(2,1)S(1)} %get-tuple-element.4), kind=kOutput, calls=%fused_computation.10 | convolution fusion | flops 44126208 | bytes 1114112 | tf_op jit(solution)/shard_map/dot_general | solution.py:37
  14.2 7.3 %all-to-all-start.1 = ((bf16[8,12,1792]{2,1,0:T(8,128)(2,1)}), bf16[8,12,1792]{2,1,0:T(8,128)(2,1)S(1)}, u32[]{:S(2)}, u32[]{:S(2)}) async-start(bf16[8,12,1792]{2,1,0:T(8,128)(2,1)} %bitcast.3), calls=%async_computation.1 | async-start | bytes 917504 | tf_op jit(solution)/shard_map/all_to_all | solution.py:44
  21.5 1.8 %convolution_convert_fusion.4 = bf16[48,1792]{1,0:T(8,128)(2,1)S(1)} fusion(f32[48,256]{1,0:T(8,128)S(1)} %get-tuple-element.5, bf16[256,1792]{1,0:T(8,128)(2,1)} %param.8), kind=kOutput, calls=%fused_computation.11 | convolution fusion | flops 264327168 | bytes 1138688 | tf_op jit(solution)/shard_map/dot_general | solution.py:38
  23.3 11.3 %all-to-all-done.1 = bf16[8,12,1792]{2,1,0:T(8,128)(2,1)S(1)} async-done(((bf16[8,12,1792]{2,1,0:T(8,128)(2,1)}), bf16[8,12,1792]{2,1,0:T(8,128)(2,1)S(1)}, u32[]{:S(2)}, u32[]{:S(2)}) %all-to-all-start.1) | async-done | bytes 344096 | tf_op jit(solution)/shard_map/all_to_all | solution.py:44
  35.4 3.6 %all-to-all-start = ((bf16[8,12,1792]{2,1,0:T(8,128)(2,1)}), bf16[8,12,1792]{2,1,0:T(8,128)(2,1)S(1)}, u32[]{:S(2)}, u32[]{:S(2)}) async-start(bf16[8,12,1792]{2,1,0:T(8,128)(2,1)} %bitcast.1), calls=%async_computation | async-start | bytes 917504 | tf_op jit(solution)/shard_map/all_to_all | solution.py:45
  39.2 1.1 fusion.20
  40.7 1.1 fusion.17
  41.8 10.3 %all-to-all-done = bf16[8,12,1792]{2,1,0:T(8,128)(2,1)S(1)} async-done(((bf16[8,12,1792]{2,1,0:T(8,128)(2,1)}), bf16[8,12,1792]{2,1,0:T(8,128)(2,1)S(1)}, u32[]{:S(2)}, u32[]{:S(2)}) %all-to-all-start) | async-done | bytes 344096 | tf_op jit(solution)/shard_map/all_to_all | solution.py:45
  52.3 2.2 %fusion.14 = bf16[96,512]{1,0:T(8,128)(2,1)S(1)} fusion(bf16[96,1792]{1,0:T(8,128)(2,1)S(1)} %reshape.59, bf16[1,512,1792]{2,1,0:T(8,128)(2,1)} %param.13), kind=kOutput, calls=%fused_computation.21 | convolution fusion | flops 176209920 | bytes 2277376 | tf_op jit(solution)/shard_map/dot_general | solution.py:57
  55.3 21.0 %all-reduce.3.cloned.1.call-done = (bf16[96,512]{1,0:T(8,128)(2,1)}, bf16[96,512]{1,0:T(8,128)(2,1)}) async-done(((bf16[96,512]{1,0:T(8,128)(2,1)}, bf16[96,512]{1,0:T(8,128)(2,1)}), (bf16[96,512]{1,0:T(8,128)(2,1)}, bf16[96,512]{1,0:T(8,128)(2,1)})) %all-reduce.3.cloned.1.call-update) | async-done | bytes 196624 | tf_op jit(solution)/shard_map/psum | solution.py:60
  76.3 0.9 convert_element_type.72
  77.2 0.9 convert_element_type.74
  78.1 20.8 %reduce-scatter.4.cloned.1.call-done = bf16[128,96]{1,0:T(8,128)(2,1)} async-done(((bf16[512,96]{1,0:T(8,128)(2,1)}), bf16[128,96]{1,0:T(8,128)(2,1)}) %reduce-scatter.4.cloned.1.call-update) | async-done | bytes 24592
  99.9 5.5 %all_gather.7 = bf16[96,512]{1,0:T(8,128)(2,1)S(1)} all-gather(bf16[96,128]{1,0:T(8,128)(2,1)S(1)} %get-tuple-element.10), channel_id=1, replica_groups=mesh['expert'=8,'fsdp'=4] {'fsdp'}, dimensions={1}, use_global_device_ids=true | all-gather | bytes 122880 | tf_op jit(solution)/shard_map/all_gather | solution.py:73
  105.3 5.3 %all_gather.6 = bf16[96,512]{1,0:T(8,128)(2,1)S(1)} all-gather(bf16[96,128]{1,0:T(8,128)(2,1)S(1)} %get-tuple-element.11), channel_id=1, replica_groups=mesh['expert'=8,'fsdp'=4] {'fsdp'}, dimensions={1}, use_global_device_ids=true | all-gather | bytes 122880 | tf_op jit(solution)/shard_map/all_gather | solution.py:72
  112.9 5.5 %all-to-all-start.2 = ((bf16[8,12,1792]{2,1,0:T(8,128)(2,1)}), bf16[8,12,1792]{2,1,0:T(8,128)(2,1)S(1)}, u32[]{:S(2)}, u32[]{:S(2)}) async-start(bf16[8,12,1792]{2,1,0:T(8,128)(2,1)} %reshape.63), calls=%async_computation.2 | async-start | bytes 917504 | tf_op jit(solution)/shard_map/all_to_all | solution.py:91
  118.5 1.9 %fusion.2 = bf16[1,512,1792]{2,1,0:T(8,128)(2,1)} fusion(bf16[96,1792]{1,0:T(8,128)(2,1)S(1)} %reshape.59, bf16[96,512]{1,0:T(8,128)(2,1)S(1)} %copy-done.4, bf16[96,512]{1,0:T(8,128)(2,1)S(1)} %copy-done.3), kind=kOutput, calls=%fused_computation.6 | convolution fusion | flops 177471488 | bytes 2375680 | tf_op jit(solution)/shard_map/dot_general | solution.py:75
  120.4 1.9 %fusion.1 = bf16[1,1792,512]{2,1,0:T(8,128)(2,1)} fusion(bf16[96,1792]{1,0:T(8,128)(2,1)S(1)} %reshape.62, bf16[96,512]{1,0:T(8,128)(2,1)S(1)} %all_gather.7), kind=kOutput, calls=%fused_computation.5 | convolution fusion | flops 177078272 | bytes 2277376 | tf_op jit(solution)/shard_map/dot_general | solution.py:81
  122.3 1.9 %fusion = bf16[1,1792,512]{2,1,0:T(8,128)(2,1)} fusion(bf16[96,1792]{1,0:T(8,128)(2,1)S(1)} %reshape.62, bf16[96,512]{1,0:T(8,128)(2,1)S(1)} %all_gather.6), kind=kOutput, calls=%fused_computation.4 | convolution fusion | flops 177078272 | bytes 2277376 | tf_op jit(solution)/shard_map/dot_general | solution.py:78
  124.2 7.9 %all-to-all-done.2 = bf16[8,12,1792]{2,1,0:T(8,128)(2,1)S(1)} async-done(((bf16[8,12,1792]{2,1,0:T(8,128)(2,1)}), bf16[8,12,1792]{2,1,0:T(8,128)(2,1)S(1)}, u32[]{:S(2)}, u32[]{:S(2)}) %all-to-all-start.2) | async-done | bytes 344096 | tf_op jit(solution)/shard_map/all_to_all | solution.py:91
  132.6 1.3 fusion.3
  (40 shorter events, 8.5 us)
Async XLA Ops:
  7.2 32.0 %copy-start = (bf16[1,1792,512]{2,1,0:T(8,128)(2,1)S(1)}, bf16[1,1792,512]{2,1,0:T(8,128)(2,1)}, u32[]{:S(2)}) copy-start(bf16[1,1792,512]{2,1,0:T(8,128)(2,1)} %param.11) | copy-start | bytes 5505028
  14.2 20.4 %all-to-all-start.1 = ((bf16[8,12,1792]{2,1,0:T(8,128)(2,1)}), bf16[8,12,1792]{2,1,0:T(8,128)(2,1)S(1)}, u32[]{:S(2)}, u32[]{:S(2)}) async-start(bf16[8,12,1792]{2,1,0:T(8,128)(2,1)} %bitcast.3), calls=%async_computation.1 | async-start | bytes 917504 | tf_op jit(solution)/shard_map/all_to_all | solution.py:44
  35.4 16.8 %all-to-all-start = ((bf16[8,12,1792]{2,1,0:T(8,128)(2,1)}), bf16[8,12,1792]{2,1,0:T(8,128)(2,1)S(1)}, u32[]{:S(2)}, u32[]{:S(2)}) async-start(bf16[8,12,1792]{2,1,0:T(8,128)(2,1)} %bitcast.1), calls=%async_computation | async-start | bytes 917504 | tf_op jit(solution)/shard_map/all_to_all | solution.py:45
  39.0 37.3 %all-reduce.3.cloned.1.call-start = ((), (), s32[]{:S(2)}) async-start(), calls=%async_computation.5 | async-start | bytes 393216 | tf_op jit(solution)/shard_map/psum | solution.py:60
  39.1 1.5 %copy-start.1 = (bf16[1,1792,512]{2,1,0:T(8,128)(2,1)S(1)}, bf16[1,1792,512]{2,1,0:T(8,128)(2,1)}, u32[]{:S(2)}) copy-start(bf16[1,1792,512]{2,1,0:T(8,128)(2,1)} %param.12) | copy-start | bytes 5505028
  41.8 57.1 %reduce-scatter.4.cloned.1.call-start = ((), (), s32[]{:S(2)}) async-start(), calls=%async_computation.4 | async-start | bytes 163840
  99.8 11.6 %copy-start.2 = (bf16[1,1792,512]{2,1,0:T(8,128)(2,1)S(1)}, bf16[1,1792,512]{2,1,0:T(8,128)(2,1)}, u32[]{:S(2)}) copy-start(bf16[1,1792,512]{2,1,0:T(8,128)(2,1)} %param.12) | copy-start | bytes 5505028
  111.4 7.1 %copy-start.3 = (bf16[96,512]{1,0:T(8,128)(2,1)S(1)}, bf16[96,512]{1,0:T(8,128)(2,1)}, u32[]{:S(2)}) copy-start(bf16[96,512]{1,0:T(8,128)(2,1)} %get-tuple-element.6) | copy-start | bytes 294916
  111.4 7.1 %copy-start.4 = (bf16[96,512]{1,0:T(8,128)(2,1)S(1)}, bf16[96,512]{1,0:T(8,128)(2,1)}, u32[]{:S(2)}) copy-start(bf16[96,512]{1,0:T(8,128)(2,1)} %get-tuple-element.7) | copy-start | bytes 294916
  112.9 19.1 %all-to-all-start.2 = ((bf16[8,12,1792]{2,1,0:T(8,128)(2,1)}), bf16[8,12,1792]{2,1,0:T(8,128)(2,1)S(1)}, u32[]{:S(2)}, u32[]{:S(2)}) async-start(bf16[8,12,1792]{2,1,0:T(8,128)(2,1)} %reshape.63), calls=%async_computation.2 | async-start | bytes 917504 | tf_op jit(solution)/shard_map/all_to_all | solution.py:91
Sparse Core Ops, SparseCore 0:
  42.7 33.5 all-reduce.2
  79.3 19.6 reduce-scatter.3
where the time goes:
time: 142 us; the launch traced here: 141 us
  waiting for transfers between devices  71.4 us (50%)
  starting transfers between devices  16.5 us (12%)
  matrix products  16.4 us (12%)
  between operations  14.2 us (10%)
  blocking collectives  10.8 us (8%)
  local copies, waits for them, and re-layouts  6.46 us (5%)
  other arithmetic  4.98 us (4%)
    psum x1, waiting for transfers between devices, body(): lax.psum(up_part.astype(jnp.bfloat16), 'fsdp').astype(jnp.float32)  21 us
    unnamed x3, waiting for transfers between devices  20.9 us
    all_to_all x1, waiting for transfers between devices, body(): lax.all_to_all(paired_rows, 'expert', split_axis=0, concat_axis=0, tiled=...  11.3 us
    all_to_all x1, waiting for transfers between devices, body(): lax.all_to_all(paired_grads, 'expert', split_axis=0, concat_axis=0, tiled...  10.3 us
    all_to_all x1, waiting for transfers between devices, body(): lax.all_to_all(back_rows.reshape(expert_count, CAP, slab_width), 'expert'...  7.87 us
    all_to_all x1, starting transfers between devices, body(): lax.all_to_all(paired_rows, 'expert', split_axis=0, concat_axis=0, tiled=...  7.28 us
    all_to_all x1, starting transfers between devices, body(): lax.all_to_all(back_rows.reshape(expert_count, CAP, slab_width), 'expert'...  5.51 us
    all_gather x1, blocking collectives, body(): lax.all_gather(up_piece, 'fsdp', axis=1, tiled=True)  5.49 us
  transfers between devices with their start and end apart: 5, of which 5 were waited for; matrix products, arithmetic and copies ran while one was open for 10% of the time, Pallas kernels for 0%

commit v1 on v0

--- a/solution.py
+++ b/solution.py
@@ -1,9 +1,35 @@
+import functools
 import jax
 import jax.numpy as jnp
 from jax import lax
 from jax.sharding import PartitionSpec as P
 
 CAP = 12
+
+
+def treat_side(mat, peer_axis):
+    tile_out = lax.axis_size(peer_axis)
+    heard = lax.axis_index(peer_axis)
+    current_value, u_next = (tile_out, heard)
+    fresh = mat.shape[0] // current_value
+    built = list(mat.shape)
+    built[0] = fresh
+    x_now = built[0]
+    built[0] = x_now * current_value
+    all_rows = jnp.zeros(built, mat.dtype)
+    for idx in range(current_value):
+        raw_out = lax.dynamic_slice_in_dim(mat, (u_next ^ idx) * fresh, fresh, axis=0)
+        if idx:
+            newest = range(current_value)
+            odd = list(map(lambda ix: (ix, ix ^ idx), newest))
+            raw_out = lax.ppermute(raw_out, peer_axis, odd)
+        all_rows = lax.dynamic_update_slice_in_dim(
+            all_rows, raw_out, (u_next ^ idx) * x_now, axis=0
+        )
+    return all_rows
+
+
+set_part = functools.partial(treat_side, peer_axis="expert")
 
 
 def swiglu_grads(gate, up_value, hidden_grad):
@@ -41,7 +67,7 @@
     paired_rows = jnp.repeat(sent_rows.reshape(window, CAP, slab_width), 2, axis=0)
     paired_grads = jnp.repeat(sent_grads.reshape(window, CAP, slab_width), 2, axis=0)
     recv_rows, recv_grads = (
-        lax.all_to_all(paired_rows, "expert", split_axis=0, concat_axis=0, tiled=True),
+        set_part(paired_rows),
         lax.all_to_all(paired_grads, "expert", split_axis=0, concat_axis=0, tiled=True),
     )
     rows = recv_rows.reshape(slot_count, slab_width)

time: 142 us -> 147 us (1.035)
  starting transfers between devices: 16.5 us -> 26.1 us
  waiting for transfers between devices: 71.4 us -> 66.1 us
    ppermute x0 -> x7, starting transfers between devices: none -> 15.6 us  [treat_side(): raw_out = lax.ppermute(raw_out, peer_axis, odd)]
    all_to_all x1 -> x0, waiting for transfers between devices: 11.3 us -> none  [body(): lax.all_to_all(paired_rows, 'expert', split_axis=0, concat_axis=0, tiled=...]
    all_to_all x1, waiting for transfers between devices: 10.3 us -> 0.01 us  [body(): lax.all_to_all(paired_grads, 'expert', split_axis=0, concat_axis=0, tiled...]
    ppermute x0 -> x7, waiting for transfers between devices: none -> 9.38 us  [treat_side(): raw_out = lax.ppermute(raw_out, peer_axis, odd)]
    all_to_all x1 -> x0, starting transfers between devices: 7.28 us -> none  [body(): lax.all_to_all(paired_rows, 'expert', split_axis=0, concat_axis=0, tiled=...]
    psum x1, waiting for transfers between devices: 21 us -> 28 us  [body(): lax.psum(up_part.astype(jnp.bfloat16), 'fsdp').astype(jnp.float32)]
  transfers between devices with their start and end apart: 5 -> 11, of which waited for: 5 -> 7; matrix products, arithmetic and copies ran while one was open for 10% -> 11% of each run, Pallas kernels for 0% -> 0%
where the time goes in v1:
time: 147 us; the launch traced here: 146 us
  waiting for transfers between devices  66.1 us (45%)
  starting transfers between devices  26.1 us (18%)
  matrix products  16.4 us (11%)
  between operations  14.4 us (10%)
  blocking collectives  10.8 us (7%)
  local copies, waits for them, and re-layouts  7.26 us (5%)
  other arithmetic  4.98 us (3%)
    psum x1, waiting for transfers between devices, body(): lax.psum(up_part.astype(jnp.bfloat16), 'fsdp').astype(jnp.float32)  28 us
    unnamed x3, waiting for transfers between devices  20.9 us
    ppermute x7, starting transfers between devices, treat_side(): raw_out = lax.ppermute(raw_out, peer_axis, odd)  15.6 us
    ppermute x7, waiting for transfers between devices, treat_side(): raw_out = lax.ppermute(raw_out, peer_axis, odd)  9.38 us
    all_to_all x1, waiting for transfers between devices, body(): lax.all_to_all(back_rows.reshape(expert_count, CAP, slab_width), 'expert'...  7.87 us
    all_to_all x1, starting transfers between devices, body(): lax.all_to_all(back_rows.reshape(expert_count, CAP, slab_width), 'expert'...  5.51 us
    all_gather x1, blocking collectives, body(): lax.all_gather(up_piece, 'fsdp', axis=1, tiled=True)  5.49 us
    all_gather x1, blocking collectives, body(): lax.all_gather(gate_piece, 'fsdp', axis=1, tiled=True)  5.34 us
  transfers between devices with their start and end apart: 11, of which 7 were waited for; matrix products, arithmetic and copies ran while one was open for 11% of the time, Pallas kernels for 0%

profile of v1, /device:TPU:0, one launch (start us, length us, event | category | flops | bytes accessed | tf_op | source)
XLA Modules:
  0.0 146.0 jit_solution(5459413489291548880)
XLA Ops:
  8.4 1.2 reduce-window.6
  11.9 1.5 %convolution_convert_fusion.3 = bf16[48,1792]{1,0:T(8,128)(2,1)S(1)} fusion(bf16[256,1792]{1,0:T(8,128)(2,1)} %param.7, bf16[48,256]{1,0:T(8,128)(2,1)S(1)} %get-tuple-element.4), kind=kOutput, calls=%fused_computation.10 | convolution fusion | flops 44126208 | bytes 1114112 | tf_op jit(solution)/shard_map/dot_general | solution.py:63
  14.2 3.0 %collective-permute-start = (bf16[1,12,1792]{2,1,0:T(8,128)(2,1)}, bf16[1,12,1792]{2,1,0:T(8,128)(2,1)}, u32[]{:S(2)}, u32[]{:S(2)}) collective-permute-start(bf16[1,12,1792]{2,1,0:T(8,128)(2,1)} %get-tuple-element.16), channel_id=1, source_target_pairs={{0,4},{4,0},{8,12},{12,8},{16,20},{20,16},{24,28},{28,24},{1,5},{5... | collective-permute-start | bytes 129032 | tf_op jit(solution)/shard_map/ppermute | solution.py:25
  17.2 1.8 %convolution_convert_fusion.4 = bf16[48,1792]{1,0:T(8,128)(2,1)S(1)} fusion(f32[48,256]{1,0:T(8,128)S(1)} %get-tuple-element.5, bf16[256,1792]{1,0:T(8,128)(2,1)} %param.8), kind=kOutput, calls=%fused_computation.11 | convolution fusion | flops 264327168 | bytes 1138688 | tf_op jit(solution)/shard_map/dot_general | solution.py:64
  19.8 4.9 %all-to-all-start = ((bf16[8,12,1792]{2,1,0:T(8,128)(2,1)}), bf16[8,12,1792]{2,1,0:T(8,128)(2,1)S(1)}, u32[]{:S(2)}, u32[]{:S(2)}) async-start(bf16[8,12,1792]{2,1,0:T(8,128)(2,1)} %bitcast.1), calls=%async_computation | async-start | bytes 917504 | tf_op jit(solution)/shard_map/all_to_all | solution.py:71
  24.7 4.7 %collective-permute-start.6 = (bf16[1,12,1792]{2,1,0:T(8,128)(2,1)S(1)}, bf16[1,12,1792]{2,1,0:T(8,128)(2,1)S(1)}, u32[]{:S(2)}, u32[]{:S(2)}) collective-permute-start(bf16[1,12,1792]{2,1,0:T(8,128)(2,1)S(1)} %get-tuple-element.10), channel_id=1, source_target_pairs={{0,28},{4,24},{8,20},{12,16},{16,12},{20,8},{24,4},{28,0},{1,29},{... | collective-permute-start | bytes 129032 | tf_op jit(solution)/shard_map/ppermute | solution.py:25
  30.5 1.9 %collective-permute-start.3 = (bf16[1,12,1792]{2,1,0:T(8,128)(2,1)S(1)}, bf16[1,12,1792]{2,1,0:T(8,128)(2,1)S(1)}, u32[]{:S(2)}, u32[]{:S(2)}) collective-permute-start(bf16[1,12,1792]{2,1,0:T(8,128)(2,1)S(1)} %get-tuple-element.13), channel_id=1, source_target_pairs={{0,16},{4,20},{8,24},{12,28},{16,0},{20,4},{24,8},{28,12},{1,17},{... | collective-permute-start | bytes 129032 | tf_op jit(solution)/shard_map/ppermute | solution.py:25
  32.4 1.4 collective-permute-start.1
  34.6 3.5 %collective-permute-done.1 = bf16[1,12,1792]{2,1,0:T(8,128)(2,1)S(1)} collective-permute-done((bf16[1,12,1792]{2,1,0:T(8,128)(2,1)S(1)}, bf16[1,12,1792]{2,1,0:T(8,128)(2,1)S(1)}, u32[]{:S(2)}, u32[]{:S(2)}) %collective-permute-start.1) | collective-permute-done | bytes 43040 | tf_op jit(solution)/shard_map/ppermute | solution.py:25
  38.2 3.6 %collective-permute-start.2 = (bf16[1,12,1792]{2,1,0:T(8,128)(2,1)S(1)}, bf16[1,12,1792]{2,1,0:T(8,128)(2,1)S(1)}, u32[]{:S(2)}, u32[]{:S(2)}) collective-permute-start(bf16[1,12,1792]{2,1,0:T(8,128)(2,1)S(1)} %get-tuple-element.14), channel_id=1, source_target_pairs={{0,12},{4,8},{8,4},{12,0},{16,28},{20,24},{24,20},{28,16},{1,13},{... | collective-permute-start | bytes 129032 | tf_op jit(solution)/shard_map/ppermute | solution.py:25
  41.7 2.7 %collective-permute-done.2 = bf16[1,12,1792]{2,1,0:T(8,128)(2,1)S(1)} collective-permute-done((bf16[1,12,1792]{2,1,0:T(8,128)(2,1)S(1)}, bf16[1,12,1792]{2,1,0:T(8,128)(2,1)S(1)}, u32[]{:S(2)}, u32[]{:S(2)}) %collective-permute-start.2) | collective-permute-done | bytes 43040 | tf_op jit(solution)/shard_map/ppermute | solution.py:25
  44.4 2.9 %collective-permute-done.3 = bf16[1,12,1792]{2,1,0:T(8,128)(2,1)S(1)} collective-permute-done((bf16[1,12,1792]{2,1,0:T(8,128)(2,1)S(1)}, bf16[1,12,1792]{2,1,0:T(8,128)(2,1)S(1)}, u32[]{:S(2)}, u32[]{:S(2)}) %collective-permute-start.3) | collective-permute-done | bytes 43040 | tf_op jit(solution)/shard_map/ppermute | solution.py:25
  47.8 1.1 fusion.20
  50.5 2.2 %fusion.14 = bf16[96,512]{1,0:T(8,128)(2,1)S(1)} fusion(bf16[96,1792]{1,0:T(8,128)(2,1)S(1)} %reshape.59, bf16[1,512,1792]{2,1,0:T(8,128)(2,1)} %param.13), kind=kOutput, calls=%fused_computation.21 | convolution fusion | flops 176209920 | bytes 2277376 | tf_op jit(solution)/shard_map/dot_general | solution.py:83
  53.5 28.0 %all-reduce.3.cloned.1.call-done = (bf16[96,512]{1,0:T(8,128)(2,1)}, bf16[96,512]{1,0:T(8,128)(2,1)}) async-done(((bf16[96,512]{1,0:T(8,128)(2,1)}, bf16[96,512]{1,0:T(8,128)(2,1)}), (bf16[96,512]{1,0:T(8,128)(2,1)}, bf16[96,512]{1,0:T(8,128)(2,1)})) %all-reduce.3.cloned.1.call-update) | async-done | bytes 196624 | tf_op jit(solution)/shard_map/psum | solution.py:86
  83.3 20.8 %reduce-scatter.4.cloned.1.call-done = bf16[128,96]{1,0:T(8,128)(2,1)} async-done(((bf16[512,96]{1,0:T(8,128)(2,1)}), bf16[128,96]{1,0:T(8,128)(2,1)}) %reduce-scatter.4.cloned.1.call-update) | async-done | bytes 24592
  105.1 5.5 %all_gather.7 = bf16[96,512]{1,0:T(8,128)(2,1)S(1)} all-gather(bf16[96,128]{1,0:T(8,128)(2,1)S(1)} %get-tuple-element.18), channel_id=1, replica_groups=mesh['expert'=8,'fsdp'=4] {'fsdp'}, dimensions={1}, use_global_device_ids=true | all-gather | bytes 122880 | tf_op jit(solution)/shard_map/all_gather | solution.py:99
  110.6 5.3 %all_gather.6 = bf16[96,512]{1,0:T(8,128)(2,1)S(1)} all-gather(bf16[96,128]{1,0:T(8,128)(2,1)S(1)} %get-tuple-element.19), channel_id=1, replica_groups=mesh['expert'=8,'fsdp'=4] {'fsdp'}, dimensions={1}, use_global_device_ids=true | all-gather | bytes 122880 | tf_op jit(solution)/shard_map/all_gather | solution.py:98
  118.2 5.5 %all-to-all-start.1 = ((bf16[8,12,1792]{2,1,0:T(8,128)(2,1)}), bf16[8,12,1792]{2,1,0:T(8,128)(2,1)S(1)}, u32[]{:S(2)}, u32[]{:S(2)}) async-start(bf16[8,12,1792]{2,1,0:T(8,128)(2,1)} %reshape.63), calls=%async_computation.1 | async-start | bytes 917504 | tf_op jit(solution)/shard_map/all_to_all | solution.py:117
  123.7 1.9 %fusion.2 = bf16[1,512,1792]{2,1,0:T(8,128)(2,1)} fusion(bf16[96,1792]{1,0:T(8,128)(2,1)S(1)} %reshape.59, bf16[96,512]{1,0:T(8,128)(2,1)S(1)} %copy-done.4, bf16[96,512]{1,0:T(8,128)(2,1)S(1)} %copy-done.3), kind=kOutput, calls=%fused_computation.6 | convolution fusion | flops 177471488 | bytes 2375680 | tf_op jit(solution)/shard_map/dot_general | solution.py:101
  125.6 1.9 %fusion.1 = bf16[1,1792,512]{2,1,0:T(8,128)(2,1)} fusion(bf16[96,1792]{1,0:T(8,128)(2,1)S(1)} %reshape.62, bf16[96,512]{1,0:T(8,128)(2,1)S(1)} %all_gather.7), kind=kOutput, calls=%fused_computation.5 | convolution fusion | flops 177078272 | bytes 2277376 | tf_op jit(solution)/shard_map/dot_general | solution.py:107
  127.5 1.9 %fusion = bf16[1,1792,512]{2,1,0:T(8,128)(2,1)} fusion(bf16[96,1792]{1,0:T(8,128)(2,1)S(1)} %reshape.62, bf16[96,512]{1,0:T(8,128)(2,1)S(1)} %all_gather.6), kind=kOutput, calls=%fused_computation.4 | convolution fusion | flops 177078272 | bytes 2277376 | tf_op jit(solution)/shard_map/dot_general | solution.py:104
  129.4 7.9 %all-to-all-done.1 = bf16[8,12,1792]{2,1,0:T(8,128)(2,1)S(1)} async-done(((bf16[8,12,1792]{2,1,0:T(8,128)(2,1)}), bf16[8,12,1792]{2,1,0:T(8,128)(2,1)S(1)}, u32[]{:S(2)}, u32[]{:S(2)}) %all-to-all-start.1) | async-done | bytes 344096 | tf_op jit(solution)/shard_map/all_to_all | solution.py:117
  137.8 1.3 fusion.3
  (61 shorter events, 15.4 us)
Async XLA Ops:
  7.2 40.6 %copy-start = (bf16[1,1792,512]{2,1,0:T(8,128)(2,1)S(1)}, bf16[1,1792,512]{2,1,0:T(8,128)(2,1)}, u32[]{:S(2)}) copy-start(bf16[1,1792,512]{2,1,0:T(8,128)(2,1)} %param.11) | copy-start | bytes 5505028
  14.2 18.2 %collective-permute-start = (bf16[1,12,1792]{2,1,0:T(8,128)(2,1)}, bf16[1,12,1792]{2,1,0:T(8,128)(2,1)}, u32[]{:S(2)}, u32[]{:S(2)}) collective-permute-start(bf16[1,12,1792]{2,1,0:T(8,128)(2,1)} %get-tuple-element.16), channel_id=1, source_target_pairs={{0,4},{4,0},{8,12},{12,8},{16,20},{20,16},{24,28},{28,24},{1,5},{5... | collective-permute-start | bytes 129032 | tf_op jit(solution)/shard_map/ppermute | solution.py:25
  19.8 30.6 %all-to-all-start = ((bf16[8,12,1792]{2,1,0:T(8,128)(2,1)}), bf16[8,12,1792]{2,1,0:T(8,128)(2,1)S(1)}, u32[]{:S(2)}, u32[]{:S(2)}) async-start(bf16[8,12,1792]{2,1,0:T(8,128)(2,1)} %bitcast.1), calls=%async_computation | async-start | bytes 917504 | tf_op jit(solution)/shard_map/all_to_all | solution.py:71
  24.7 56.8 %all-reduce.3.cloned.1.call-start = ((), (), s32[]{:S(2)}) async-start(), calls=%async_computation.4 | async-start | bytes 393216 | tf_op jit(solution)/shard_map/psum | solution.py:86
  24.7 22.9 %collective-permute-start.6 = (bf16[1,12,1792]{2,1,0:T(8,128)(2,1)S(1)}, bf16[1,12,1792]{2,1,0:T(8,128)(2,1)S(1)}, u32[]{:S(2)}, u32[]{:S(2)}) collective-permute-start(bf16[1,12,1792]{2,1,0:T(8,128)(2,1)S(1)} %get-tuple-element.10), channel_id=1, source_target_pairs={{0,28},{4,24},{8,20},{12,16},{16,12},{20,8},{24,4},{28,0},{1,29},{... | collective-permute-start | bytes 129032 | tf_op jit(solution)/shard_map/ppermute | solution.py:25
  29.4 18.2 %collective-permute-start.5 = (bf16[1,12,1792]{2,1,0:T(8,128)(2,1)S(1)}, bf16[1,12,1792]{2,1,0:T(8,128)(2,1)S(1)}, u32[]{:S(2)}, u32[]{:S(2)}) collective-permute-start(bf16[1,12,1792]{2,1,0:T(8,128)(2,1)S(1)} %get-tuple-element.11), channel_id=1, source_target_pairs={{0,24},{4,28},{8,16},{12,20},{16,8},{20,12},{24,0},{28,4},{1,25},{... | collective-permute-start | bytes 129032 | tf_op jit(solution)/shard_map/ppermute | solution.py:25
  30.0 17.6 %collective-permute-start.4 = (bf16[1,12,1792]{2,1,0:T(8,128)(2,1)S(1)}, bf16[1,12,1792]{2,1,0:T(8,128)(2,1)S(1)}, u32[]{:S(2)}, u32[]{:S(2)}) collective-permute-start(bf16[1,12,1792]{2,1,0:T(8,128)(2,1)S(1)} %get-tuple-element.12), channel_id=1, source_target_pairs={{0,20},{4,16},{8,28},{12,24},{16,4},{20,0},{24,12},{28,8},{1,21},{... | collective-permute-start | bytes 129032 | tf_op jit(solution)/shard_map/ppermute | solution.py:25
  30.5 16.8 %collective-permute-start.3 = (bf16[1,12,1792]{2,1,0:T(8,128)(2,1)S(1)}, bf16[1,12,1792]{2,1,0:T(8,128)(2,1)S(1)}, u32[]{:S(2)}, u32[]{:S(2)}) collective-permute-start(bf16[1,12,1792]{2,1,0:T(8,128)(2,1)S(1)} %get-tuple-element.13), channel_id=1, source_target_pairs={{0,16},{4,20},{8,24},{12,28},{16,0},{20,4},{24,8},{28,12},{1,17},{... | collective-permute-start | bytes 129032 | tf_op jit(solution)/shard_map/ppermute | solution.py:25
  32.4 5.7 %collective-permute-start.1 = (bf16[1,12,1792]{2,1,0:T(8,128)(2,1)S(1)}, bf16[1,12,1792]{2,1,0:T(8,128)(2,1)S(1)}, u32[]{:S(2)}, u32[]{:S(2)}) collective-permute-start(bf16[1,12,1792]{2,1,0:T(8,128)(2,1)S(1)} %get-tuple-element.15), channel_id=1, source_target_pairs={{0,8},{4,12},{8,0},{12,4},{16,24},{20,28},{24,16},{28,20},{1,9},{5... | collective-permute-start | bytes 129032 | tf_op jit(solution)/shard_map/ppermute | solution.py:25
  38.2 6.3 %collective-permute-start.2 = (bf16[1,12,1792]{2,1,0:T(8,128)(2,1)S(1)}, bf16[1,12,1792]{2,1,0:T(8,128)(2,1)S(1)}, u32[]{:S(2)}, u32[]{:S(2)}) collective-permute-start(bf16[1,12,1792]{2,1,0:T(8,128)(2,1)S(1)} %get-tuple-element.14), channel_id=1, source_target_pairs={{0,12},{4,8},{8,4},{12,0},{16,28},{20,24},{24,20},{28,16},{1,13},{... | collective-permute-start | bytes 129032 | tf_op jit(solution)/shard_map/ppermute | solution.py:25
  47.8 1.5 %copy-start.1 = (bf16[1,1792,512]{2,1,0:T(8,128)(2,1)S(1)}, bf16[1,1792,512]{2,1,0:T(8,128)(2,1)}, u32[]{:S(2)}) copy-start(bf16[1,1792,512]{2,1,0:T(8,128)(2,1)} %param.12) | copy-start | bytes 5505028
  50.4 53.8 %reduce-scatter.4.cloned.1.call-start = ((), (), s32[]{:S(2)}) async-start(), calls=%async_computation.3 | async-start | bytes 163840
  105.0 11.6 %copy-start.2 = (bf16[1,1792,512]{2,1,0:T(8,128)(2,1)S(1)}, bf16[1,1792,512]{2,1,0:T(8,128)(2,1)}, u32[]{:S(2)}) copy-start(bf16[1,1792,512]{2,1,0:T(8,128)(2,1)} %param.12) | copy-start | bytes 5505028
  116.6 7.1 %copy-start.3 = (bf16[96,512]{1,0:T(8,128)(2,1)S(1)}, bf16[96,512]{1,0:T(8,128)(2,1)}, u32[]{:S(2)}) copy-start(bf16[96,512]{1,0:T(8,128)(2,1)} %get-tuple-element.6) | copy-start | bytes 294916
  116.6 7.1 %copy-start.4 = (bf16[96,512]{1,0:T(8,128)(2,1)S(1)}, bf16[96,512]{1,0:T(8,128)(2,1)}, u32[]{:S(2)}) copy-start(bf16[96,512]{1,0:T(8,128)(2,1)} %get-tuple-element.7) | copy-start | bytes 294916
  118.2 19.1 %all-to-all-start.1 = ((bf16[8,12,1792]{2,1,0:T(8,128)(2,1)}), bf16[8,12,1792]{2,1,0:T(8,128)(2,1)S(1)}, u32[]{:S(2)}, u32[]{:S(2)}) async-start(bf16[8,12,1792]{2,1,0:T(8,128)(2,1)} %reshape.63), calls=%async_computation.1 | async-start | bytes 917504 | tf_op jit(solution)/shard_map/all_to_all | solution.py:117
Sparse Core Ops, SparseCore 0:
  50.5 30.9 all-reduce.2
  84.5 19.6 reduce-scatter.3
